TPU v7x, 128 devices: a whole 4x4x4 slice. The times are simulated.
128 devices in a mesh: batch: 8 (over x, core), item: 16 (over z, y).
Axes of the slice: x: 4, y: 4, z: 4, core: 2. Of those that a mesh axis runs over, the one named last changes fastest.
Arguments:
- user_vectors: bfloat16 [32768, 512], P(('batch', 'item')), may hold values from -6 to 6
- item_table: bfloat16 [524288, 512], P(('batch', 'item')), may hold values from -0.25 to 0.25
- tower_weight: bfloat16 [512, 512], replicated, may hold values from -3 to 3
- item_owner: int32 [32768, 1], P(('batch', 'item')), may hold values from 0 to 127; in each aligned block of 256 rows (0 to 255, 256 to 511, ...) at most 4 rows name the same one
- item_row: int32 [32768], P(('batch', 'item')), may hold values from 0 to 4095
Outputs:
- table_grad: bfloat16 [524288, 512], P(('batch', 'item'))
- weight_grad: float32 [512, 512], P(('batch', 'item'))
Inputs may be any that keep to these rules, and one draw needn't show every extreme that they name: `item_owner`: within the rows of one device (aligned blocks of 256 rows) no owner is named by more than 4 rows, a bound that some block reaches.
All inputs are finite; a program needn't handle non-finite values.
Results may differ from a plain program's by a relative error of at most 0.0075.
Values may be sent and summed in bfloat16 or wider, within the bound.
A program may use at most 64 MiB of HBM per device.

v0:
```python
import jax
import jax.numpy as jnp
from jax import lax
from jax.sharding import PartitionSpec as P

epsilon = 1e-06
score_scale = 60.0
cauchy_scale = 4.0


def local(user_vectors, item_table, tower_weight, item_owner, item_row):
    b_dev, width = user_vectors.shape
    n_batch = lax.axis_size("batch")
    n_item = lax.axis_size("item")
    devices = n_batch * n_item
    slots = 2 * b_dev // devices
    owner = item_owner[:, 0]
    onehot = (owner[:, None] == jnp.arange(devices, dtype=jnp.int32)[None, :]).astype(jnp.int32)
    rank = jnp.sum(jnp.cumsum(onehot, axis=0) * onehot, axis=1) - 1
    place = owner * slots + rank
    request = (
        jnp.zeros((devices * slots,), jnp.int32).at[place].set(item_row).reshape(devices, slots)
    )
    asked = lax.all_to_all(request, ("batch", "item"), split_axis=0, concat_axis=0, tiled=True)
    found = item_table[asked]
    back = lax.all_to_all(found, ("batch", "item"), split_axis=0, concat_axis=0, tiled=True)
    fetched, asked = (back, asked)
    embed = fetched.reshape(devices * slots, width)[place]
    hidden = jnp.dot(embed, tower_weight, preferred_element_type=jnp.float32)
    rscale = lax.rsqrt(jnp.mean(hidden * hidden, axis=1, keepdims=True) + epsilon)
    item_vec = (hidden * rscale / jnp.sqrt(jnp.float32(width))).astype(jnp.bfloat16)
    user_f = user_vectors.astype(jnp.float32)
    user_unit = (
        user_f
        * lax.rsqrt(jnp.mean(user_f * user_f, axis=1, keepdims=True) + epsilon)
        / jnp.sqrt(jnp.float32(width))
    ).astype(jnp.bfloat16)
    piece = lax.all_gather(user_unit, "batch", axis=0, tiled=True)
    score = (
        lax.dot_general(
            item_vec, piece, (((1,), (1,)), ((), ())), preferred_element_type=jnp.float32
        )
        * score_scale
    )
    expo = jnp.exp(score)
    partial_mix = jnp.dot(expo.astype(jnp.bfloat16), piece, preferred_element_type=jnp.float32)
    total = jnp.sum(expo, axis=1)
    unit_f = user_unit.astype(jnp.float32)
    positive = jnp.sum(item_vec.astype(jnp.float32) * unit_f, axis=1) * score_scale
    xent = jnp.log(total) - positive
    cweight = 1.0 / (1.0 + xent / cauchy_scale)
    dvec = cweight[:, None] * score_scale * (partial_mix / total[:, None] - unit_f)
    inner = jnp.sum(hidden * dvec, axis=1, keepdims=True)
    dhidden = (
        rscale / jnp.sqrt(jnp.float32(width)) * (dvec - hidden * rscale * rscale * inner / width)
    ).astype(jnp.bfloat16)
    weight_grad = lax.psum_scatter(
        lax.dot_general(
            embed, dhidden, (((0,), (0,)), ((), ())), preferred_element_type=jnp.float32
        ),
        ("batch", "item"),
        scatter_dimension=0,
        tiled=True,
    )
    drow = jnp.dot(dhidden, tower_weight.T, preferred_element_type=jnp.float32)
    outgoing = jnp.zeros((devices * slots, width), jnp.float32).at[place].set(drow)
    incoming = lax.all_to_all(
        outgoing.reshape(devices, slots, width).astype(jnp.bfloat16),
        ("batch", "item"),
        split_axis=0,
        concat_axis=0,
        tiled=True,
    ).astype(jnp.float32)
    arrived = incoming.reshape(devices * slots, width)
    table_grad = (
        jnp.zeros((item_table.shape[0], width), jnp.float32).at[asked.reshape(-1)].add(arrived)
    )
    return (table_grad.astype(jnp.bfloat16), weight_grad)


def solution(mesh):
    return jax.shard_map(
        local,
        mesh=mesh,
        in_specs=(
            P(("batch", "item"), None),
            P(("batch", "item"), None),
            P(),
            P(("batch", "item"), None),
            P(("batch", "item")),
        ),
        out_specs=(P(("batch", "item"), None), P(("batch", "item"), None)),
        check_vma=False,
    )
```

profile of v0, /device:TPU:1, one launch (start us, length us, event | category | flops | bytes accessed | tf_op | source)
XLA Modules:
  0.0 245.3 jit_solution(17994513546542418527)
XLA Ops:
  7.2 0.0 copy-start
  7.2 0.8 copy.10
  8.0 0.2 fusion.12
  8.3 0.9 fusion.13
  9.2 0.7 compare_select_fusion.2
  9.9 1.6 scatter_custom_fusion
  11.4 0.1 all_to_all.14
  11.6 21.1 %all_to_all.22 = s32[128,1,4]{2,1,0:T(1,128)S(1)} all-to-all(s32[128,1,4]{2,1,0:T(1,128)S(1)} %bitcast.34), channel_id=1, replica_groups=mesh['batch'=8,'item'=16] {'batch','item'}, dimensions={0} | all-to-all | bytes 4096 | tf_op jit(solution)/shard_map/all_to_all | solution.py:24
  32.7 0.1 reshape.147
  32.8 4.7 %gather_fusion = bf16[512,512]{1,0:T(8,128)(2,1)S(1)} fusion(bf16[4096,512]{1,0:T(8,128)(2,1)} %param.6, s32[1024]{0:T(1024)S(1)} %pad_clamp_fusion.1), kind=kCustom, calls=%fused_computation | custom fusion | bytes 1050624 | tf_op jit(solution)/shard_map/gather | solution.py:25
  37.5 0.0 copy-start.1
  37.5 0.9 reshape.146
  38.4 4.3 %all-to-all-start.1 = ((bf16[128,4,512]{2,1,0:T(4,128)(2,1)}), bf16[128,4,512]{2,1,0:T(4,128)(2,1)S(1)}, u32[]{:S(2)}, u32[]{:S(2)}) async-start(bf16[128,4,512]{2,1,0:T(4,128)(2,1)} %reshape.146), calls=%async_computation.1 | async-start | bytes 1048576 | tf_op jit(solution)/shard_map/all_to_all | solution.py:26
  42.7 0.0 all-gather.2.cloned.1.call-start
  42.8 0.0 copy-done.1
  42.8 0.1 fusion.6
  42.9 13.9 %all-to-all-done.1 = bf16[128,4,512]{2,1,0:T(4,128)(2,1)S(1)} async-done(((bf16[128,4,512]{2,1,0:T(4,128)(2,1)}), bf16[128,4,512]{2,1,0:T(4,128)(2,1)S(1)}, u32[]{:S(2)}, u32[]{:S(2)}) %all-to-all-start.1) | async-done | bytes 524320 | tf_op jit(solution)/shard_map/all_to_all | solution.py:26
  56.8 0.1 reshape.140
  57.0 1.2 gather_fusion.1
  58.1 0.0 copy-done
  58.1 0.4 multiply_reduce_fusion.1
  58.5 0.9 fusion.9
  59.4 0.0 all-gather.2.cloned.1.call-update
  59.4 0.0 copy-start.2
  59.5 0.0 all-reduce.3.cloned.1.call-start
  59.5 21.4 %all-gather.2.cloned.1.call-done = bf16[2048,512]{1,0:T(8,128)(2,1)} async-done(((bf16[256,512]{1,0:T(8,128)(2,1)}), bf16[2048,512]{1,0:T(8,128)(2,1)}) %all-gather.2.cloned.1.call-update) | async-done | bytes 2097168 | tf_op jit(solution)/shard_map/all_gather | solution.py:38
  80.9 0.0 copy-start.3
  80.9 2.6 %fusion.19 = (f32[256]{0:T(256)S(1)}, bf16[256,2048]{1,0:T(8,128)(2,1)S(1)}) fusion(bf16[2048,512]{1,0:T(8,128)(2,1)} %all-gather.2.cloned.1.call-done, f32[256,512]{1,0:T(8,128)S(1)} %get-tuple-element.7, f32[256]{0:T(256)S(1)} %get-tuple-element.5), kind=kOutput, calls=%fused_computation.48 | convolution fusion | flops 538836736 | bytes 3672064 | tf_op jit(solution)/shard_map/dot_general | solution.py:40
  83.6 0.0 copy-done.2
  83.6 0.0 copy-done.3
  83.6 0.8 multiply_reduce_fusion
  84.4 0.2 multiply_convert_fusion
  84.6 1.3 fusion.21
  85.9 0.0 all-reduce.3.cloned.1.call-update
  85.9 0.3 fusion.20
  86.3 1.7 scatter_custom_fusion.1
  88.0 0.1 convert_element_type.44
  88.0 0.9 convert_element_type.45
  88.9 8.3 %all-to-all-start.2 = ((bf16[128,4,512]{2,1,0:T(4,128)(2,1)}), bf16[128,4,512]{2,1,0:T(4,128)(2,1)S(1)}, u32[]{:S(2)}, u32[]{:S(2)}) async-start(bf16[128,4,512]{2,1,0:T(4,128)(2,1)} %convert_element_type.45), calls=%async_computation.2 | async-start | bytes 1048576 | tf_op jit(solution)/shard_map/all_to_all | solution.py:67
  97.3 0.5 broadcast.185
  97.8 0.8 reduce.3
  98.6 0.1 reshape.139
  98.7 12.9 %all-to-all-done.2 = bf16[128,4,512]{2,1,0:T(4,128)(2,1)S(1)} async-done(((bf16[128,4,512]{2,1,0:T(4,128)(2,1)}), bf16[128,4,512]{2,1,0:T(4,128)(2,1)S(1)}, u32[]{:S(2)}, u32[]{:S(2)}) %all-to-all-start.2) | async-done | bytes 524320 | tf_op jit(solution)/shard_map/all_to_all | solution.py:67
  111.6 0.1 reshape.181
  111.7 7.3 %scatter_custom_fusion.2 = f32[4096,512]{1,0:T(8,128)} fusion(s32[512]{0:T(512)S(1)} %bitcast.42, f32[512,512]{1,0:T(8,128)S(1)} %reshape.181, f32[]{:T(128)} %constant.12.clone.1), kind=kCustom, calls=%fused_computation.5 | custom fusion | flops 262144 | bytes 8388612 | tf_op jit(solution)/shard_map/scatter-add | solution.py:76
  119.0 6.0 %convert_element_type.46 = bf16[4096,512]{1,0:T(8,128)(2,1)} convert(f32[4096,512]{1,0:T(8,128)} %scatter_custom_fusion.2) | non-fusion elementwise | flops 2097152 | bytes 12582912 | tf_op jit(solution)/shard_map/convert_element_type | solution.py:78
  125.0 112.2 %all-reduce.3.cloned.1.call-done = f32[512,512]{1,0:T(8,128)} async-done(((f32[512,512]{1,0:T(8,128)}), f32[512,512]{1,0:T(8,128)}) %all-reduce.3.cloned.1.call-update) | async-done | bytes 1048592
  237.2 1.3 constant_dynamic-slice_fusion
  (13 shorter events, 0.1 us)
Async XLA Ops:
  7.2 50.9 %copy-start = (bf16[512,512]{1,0:T(8,128)(2,1)S(1)}, bf16[512,512]{1,0:T(8,128)(2,1)}, u32[]{:S(2)}) copy-start(bf16[512,512]{1,0:T(8,128)(2,1)} %param.7) | copy-start | bytes 1572868
  37.5 5.3 %copy-start.1 = (bf16[256,512]{1,0:T(8,128)(2,1)S(1)}, bf16[256,512]{1,0:T(8,128)(2,1)}, u32[]{:S(2)}) copy-start(bf16[256,512]{1,0:T(8,128)(2,1)} %param.5) | copy-start | bytes 786436
  38.4 18.4 %all-to-all-start.1 = ((bf16[128,4,512]{2,1,0:T(4,128)(2,1)}), bf16[128,4,512]{2,1,0:T(4,128)(2,1)S(1)}, u32[]{:S(2)}, u32[]{:S(2)}) async-start(bf16[128,4,512]{2,1,0:T(4,128)(2,1)} %reshape.146), calls=%async_computation.1 | async-start | bytes 1048576 | tf_op jit(solution)/shard_map/all_to_all | solution.py:26
  42.7 38.2 %all-gather.2.cloned.1.call-start = ((), (), s32[]{:S(2)}) async-start(), calls=%async_computation.3 | async-start | bytes 2359296 | tf_op jit(solution)/shard_map/all_gather | solution.py:38
  59.4 24.1 %copy-start.2 = (bf16[256,512]{1,0:T(8,128)(2,1)S(1)}, bf16[256,512]{1,0:T(8,128)(2,1)}, u32[]{:S(2)}) copy-start(bf16[256,512]{1,0:T(8,128)(2,1)} %get-tuple-element.3) | copy-start | bytes 786436
  59.5 177.7 %all-reduce.3.cloned.1.call-start = ((), (), s32[]{:S(2)}) async-start(), calls=%async_computation.4 | async-start | bytes 2097152
  80.9 2.6 %copy-start.3 = (bf16[2048,512]{1,0:T(8,128)(2,1)S(1)}, bf16[2048,512]{1,0:T(8,128)(2,1)}, u32[]{:S(2)}) copy-start(bf16[2048,512]{1,0:T(8,128)(2,1)} %all-gather.2.cloned.1.call-done) | copy-start | bytes 6291460
  88.9 22.7 %all-to-all-start.2 = ((bf16[128,4,512]{2,1,0:T(4,128)(2,1)}), bf16[128,4,512]{2,1,0:T(4,128)(2,1)S(1)}, u32[]{:S(2)}, u32[]{:S(2)}) async-start(bf16[128,4,512]{2,1,0:T(4,128)(2,1)} %convert_element_type.45), calls=%async_computation.2 | async-start | bytes 1048576 | tf_op jit(solution)/shard_map/all_to_all | solution.py:67
Sparse Core Ops, SparseCore 0:
  59.6 21.3 all-gather.1
  86.1 151.0 all-reduce.2
where the time goes:
time: 246 us; the launch traced here: 245 us
  waiting for transfers between devices  160 us (65%)
  blocking collectives  21.1 us (9%)
  other arithmetic  17.2 us (7%)
  between operations  14.3 us (6%)
  local copies, waits for them, and re-layouts  14.2 us (6%)
  starting transfers between devices  12.7 us (5%)
  matrix products  5.44 us (2%)
    unnamed x3, waiting for transfers between devices  112 us
    all_gather x1, waiting for transfers between devices, local(): piece = lax.all_gather(user_unit, 'batch', axis=0, tiled=True)  21.4 us
    all_to_all x1, blocking collectives, local(): lax.all_to_all(request, ('batch', 'item'), split_axis=0, concat_axis=0, t...  21.1 us
    all_to_all x1, waiting for transfers between devices, local(): lax.all_to_all(found, ('batch', 'item'), split_axis=0, concat_axis=0, til...  13.9 us
    all_to_all x1, waiting for transfers between devices, local(): lax.all_to_all(outgoing.reshape(devices, slots, width).astype(jnp.bfloat1...  12.9 us
    all_to_all x1, starting transfers between devices, local(): lax.all_to_all(outgoing.reshape(devices, slots, width).astype(jnp.bfloat1...  8.31 us
    scatter-add x1, other arithmetic, local(): jnp.zeros((item_table.shape[0], width), jnp.float32).at[asked.reshape(-1)]  7.29 us
    convert_element_type x1, other arithmetic, local(): return (table_grad.astype(jnp.bfloat16), weight_grad)  6 us
  transfers between devices with their start and end apart: 4, of which 4 were waited for; matrix products, arithmetic and copies ran while one was open for 7% of the time, Pallas kernels for 0%

commit v1 on v0

--- a/solution.py
+++ b/solution.py
@@ -6,6 +6,12 @@
 epsilon = 1e-06
 score_scale = 60.0
 cauchy_scale = 4.0
+
+
+def gather_from_all(x, axis, dim):
+    size = lax.axis_size(axis)
+    repeats = [size if d == dim else 1 for d in range(x.ndim)]
+    return lax.all_to_all(jnp.tile(x, repeats), axis, split_axis=dim, concat_axis=dim, tiled=True)
 
 
 def local(user_vectors, item_table, tower_weight, item_owner, item_row):
@@ -35,7 +41,7 @@
         * lax.rsqrt(jnp.mean(user_f * user_f, axis=1, keepdims=True) + epsilon)
         / jnp.sqrt(jnp.float32(width))
     ).astype(jnp.bfloat16)
-    piece = lax.all_gather(user_unit, "batch", axis=0, tiled=True)
+    piece = gather_from_all(user_unit, "batch", 0)
     score = (
         lax.dot_general(
             item_vec, piece, (((1,), (1,)), ((), ())), preferred_element_type=jnp.float32

time: 246 us -> 248 us (level)
  blocking collectives: 21.1 us -> 50.3 us
  waiting for transfers between devices: 160 us -> 139 us
  starting transfers between devices: 12.7 us -> 8.78 us
    all_to_all x0 -> x1, blocking collectives: none -> 29.2 us  [gather_from_all(): lax.all_to_all(jnp.tile(x, repeats), axis, split_axis=dim, concat_axis=di...]
    all_gather x1 -> x0, waiting for transfers between devices: 21.4 us -> none  [local(): piece = lax.all_gather(user_unit, 'batch', axis=0, tiled=True)]
    all_to_all x1, starting transfers between devices: 8.31 us -> 4.46 us  [local(): lax.all_to_all(outgoing.reshape(devices, slots, width).astype(jnp.bfloat1...]
    unnamed x3 -> x2, waiting for transfers between devices: 112 us -> 112 us
  transfers between devices with their start and end apart: 4 -> 3, of which waited for: 4 -> 3; matrix products, arithmetic and copies ran while one was open for 7% -> 7% of each run, Pallas kernels for 0% -> 0%
where the time goes in v1:
time: 248 us; the launch traced here: 247 us
  waiting for transfers between devices  139 us (56%)
  blocking collectives  50.3 us (20%)
  other arithmetic  16.6 us (7%)
  local copies, waits for them, and re-layouts  14.3 us (6%)
  between operations  14.2 us (6%)
  starting transfers between devices  8.78 us (4%)
  matrix products  3.74 us (2%)
    unnamed x2, waiting for transfers between devices  112 us
    all_to_all x1, blocking collectives, gather_from_all(): lax.all_to_all(jnp.tile(x, repeats), axis, split_axis=dim, concat_axis=di...  29.2 us
    all_to_all x1, blocking collectives, local(): lax.all_to_all(request, ('batch', 'item'), split_axis=0, concat_axis=0, t...  21.1 us
    all_to_all x1, waiting for transfers between devices, local(): lax.all_to_all(found, ('batch', 'item'), split_axis=0, concat_axis=0, til...  13.9 us
    all_to_all x1, waiting for transfers between devices, local(): lax.all_to_all(outgoing.reshape(devices, slots, width).astype(jnp.bfloat1...  13 us
    scatter-add x1, other arithmetic, local(): jnp.zeros((item_table.shape[0], width), jnp.float32).at[asked.reshape(-1)]  7.29 us
    convert_element_type x1, other arithmetic, local(): return (table_grad.astype(jnp.bfloat16), weight_grad)  5.99 us
    gather x2, local copies, waits for them, and re-layouts, local(): found = item_table[asked]  5.63 us
  transfers between devices with their start and end apart: 3, of which 3 were waited for; matrix products, arithmetic and copies ran while one was open for 7% of the time, Pallas kernels for 0%

profile of v1, /device:TPU:1, one launch (start us, length us, event | category | flops | bytes accessed | tf_op | source)
XLA Modules:
  0.0 247.1 jit_solution(1646012434362527958)
XLA Ops:
  7.2 0.0 copy-start
  7.2 0.8 copy.10
  8.0 0.2 fusion.12
  8.3 0.9 fusion.13
  9.2 0.7 compare_select_fusion.2
  9.9 1.6 scatter_custom_fusion
  11.4 0.1 all_to_all.20
  11.6 21.1 %all_to_all.31 = s32[128,1,4]{2,1,0:T(1,128)S(1)} all-to-all(s32[128,1,4]{2,1,0:T(1,128)S(1)} %bitcast.37), channel_id=1, replica_groups=mesh['batch'=8,'item'=16] {'batch','item'}, dimensions={0} | all-to-all | bytes 4096 | tf_op jit(solution)/shard_map/all_to_all | solution.py:30
  32.7 0.1 reshape.154
  32.8 4.7 %gather_fusion = bf16[512,512]{1,0:T(8,128)(2,1)S(1)} fusion(bf16[4096,512]{1,0:T(8,128)(2,1)} %param.6, s32[1024]{0:T(1024)S(1)} %pad_clamp_fusion.1), kind=kCustom, calls=%fused_computation | custom fusion | bytes 1050624 | tf_op jit(solution)/shard_map/gather | solution.py:31
  37.5 0.0 copy-start.1
  37.5 0.9 reshape.153
  38.4 4.3 %all-to-all-start.1 = ((bf16[128,4,512]{2,1,0:T(4,128)(2,1)}), bf16[128,4,512]{2,1,0:T(4,128)(2,1)S(1)}, u32[]{:S(2)}, u32[]{:S(2)}) async-start(bf16[128,4,512]{2,1,0:T(4,128)(2,1)} %reshape.153), calls=%async_computation.1 | async-start | bytes 1048576 | tf_op jit(solution)/shard_map/all_to_all | solution.py:32
  42.7 0.0 all-reduce.3.cloned.1.call-start
  42.8 0.0 copy-done.1
  42.8 0.1 fusion.6
  42.9 13.9 %all-to-all-done.1 = bf16[128,4,512]{2,1,0:T(4,128)(2,1)S(1)} async-done(((bf16[128,4,512]{2,1,0:T(4,128)(2,1)}), bf16[128,4,512]{2,1,0:T(4,128)(2,1)S(1)}, u32[]{:S(2)}, u32[]{:S(2)}) %all-to-all-start.1) | async-done | bytes 524320 | tf_op jit(solution)/shard_map/all_to_all | solution.py:32
  56.8 0.1 reshape.147
  57.0 1.2 gather_fusion.1
  58.1 0.0 copy-done
  58.1 0.4 multiply_reduce_fusion.1
  58.5 0.3 fusion.9
  58.8 0.2 tile.2
  59.0 29.2 %all_to_all.32 = bf16[8,256,512]{2,1,0:T(8,128)(2,1)S(1)} all-to-all(bf16[8,256,512]{2,1,0:T(8,128)(2,1)S(1)} %tile.2), channel_id=1, replica_groups=mesh['batch'=8,'item'=16] {'batch'}, dimensions={0} | all-to-all | bytes 4194304 | tf_op jit(solution)/shard_map/all_to_all | solution.py:14
  88.2 0.9 fusion.19
  89.1 0.9 multiply_reduce_fusion
  89.9 0.2 multiply_convert_fusion
  90.1 1.3 fusion.21
  91.4 0.0 all-reduce.3.cloned.1.call-update
  91.5 0.3 fusion.20
  91.8 1.7 scatter_custom_fusion.1
  93.5 0.1 convert_element_type.44
  93.6 0.9 convert_element_type.45
  94.5 4.5 %all-to-all-start.3 = ((bf16[128,4,512]{2,1,0:T(4,128)(2,1)}), bf16[128,4,512]{2,1,0:T(4,128)(2,1)S(1)}, u32[]{:S(2)}, u32[]{:S(2)}) async-start(bf16[128,4,512]{2,1,0:T(4,128)(2,1)} %convert_element_type.45), calls=%async_computation.3 | async-start | bytes 1048576 | tf_op jit(solution)/shard_map/all_to_all | solution.py:73
  98.9 0.5 broadcast.188
  99.5 0.8 reduce.3
  100.3 0.1 reshape.146
  100.4 13.0 %all-to-all-done.3 = bf16[128,4,512]{2,1,0:T(4,128)(2,1)S(1)} async-done(((bf16[128,4,512]{2,1,0:T(4,128)(2,1)}), bf16[128,4,512]{2,1,0:T(4,128)(2,1)S(1)}, u32[]{:S(2)}, u32[]{:S(2)}) %all-to-all-start.3) | async-done | bytes 524320 | tf_op jit(solution)/shard_map/all_to_all | solution.py:73
  113.4 0.1 reshape.188
  113.5 7.3 %scatter_custom_fusion.2 = f32[4096,512]{1,0:T(8,128)} fusion(s32[512]{0:T(512)S(1)} %bitcast.45, f32[512,512]{1,0:T(8,128)S(1)} %reshape.188, f32[]{:T(128)} %constant.12.clone.1), kind=kCustom, calls=%fused_computation.5 | custom fusion | flops 262144 | bytes 8388612 | tf_op jit(solution)/shard_map/scatter-add | solution.py:82
  120.7 6.0 %convert_element_type.46 = bf16[4096,512]{1,0:T(8,128)(2,1)} convert(f32[4096,512]{1,0:T(8,128)} %scatter_custom_fusion.2) | non-fusion elementwise | flops 2097152 | bytes 12582912 | tf_op jit(solution)/shard_map/convert_element_type | solution.py:84
  126.7 112.2 %all-reduce.3.cloned.1.call-done = f32[512,512]{1,0:T(8,128)} async-done(((f32[512,512]{1,0:T(8,128)}), f32[512,512]{1,0:T(8,128)}) %all-reduce.3.cloned.1.call-update) | async-done | bytes 1048592
  239.0 1.3 constant_dynamic-slice_fusion
  (13 shorter events, 0.1 us)
Async XLA Ops:
  7.2 50.9 %copy-start = (bf16[512,512]{1,0:T(8,128)(2,1)S(1)}, bf16[512,512]{1,0:T(8,128)(2,1)}, u32[]{:S(2)}) copy-start(bf16[512,512]{1,0:T(8,128)(2,1)} %param.7) | copy-start | bytes 1572868
  37.5 5.3 %copy-start.1 = (bf16[256,512]{1,0:T(8,128)(2,1)S(1)}, bf16[256,512]{1,0:T(8,128)(2,1)}, u32[]{:S(2)}) copy-start(bf16[256,512]{1,0:T(8,128)(2,1)} %param.5) | copy-start | bytes 786436
  38.4 18.4 %all-to-all-start.1 = ((bf16[128,4,512]{2,1,0:T(4,128)(2,1)}), bf16[128,4,512]{2,1,0:T(4,128)(2,1)S(1)}, u32[]{:S(2)}, u32[]{:S(2)}) async-start(bf16[128,4,512]{2,1,0:T(4,128)(2,1)} %reshape.153), calls=%async_computation.1 | async-start | bytes 1048576 | tf_op jit(solution)/shard_map/all_to_all | solution.py:32
  42.7 196.3 %all-reduce.3.cloned.1.call-start = ((), (), s32[]{:S(2)}) async-start(), calls=%async_computation.4 | async-start | bytes 2097152
  94.5 18.9 %all-to-all-start.3 = ((bf16[128,4,512]{2,1,0:T(4,128)(2,1)}), bf16[128,4,512]{2,1,0:T(4,128)(2,1)S(1)}, u32[]{:S(2)}, u32[]{:S(2)}) async-start(bf16[128,4,512]{2,1,0:T(4,128)(2,1)} %convert_element_type.45), calls=%async_computation.3 | async-start | bytes 1048576 | tf_op jit(solution)/shard_map/all_to_all | solution.py:73
Sparse Core Ops, SparseCore 0:
  91.6 147.3 all-reduce.2
